TPU v7x, 512 devices: a whole 4x8x8 slice. The times are simulated.
512 devices in a mesh: section: 2 (over core), sy: 8 (over y), sx: 8 (over z), mb: 4 (over x).
Axes of the slice: x: 4, y: 8, z: 8, core: 2. Of those that a mesh axis runs over, the one named last changes fastest.
Arguments:
- frames: bfloat16 [4, 512, 512, 128], P('mb', 'sy', 'sx'), may hold values from -6 to 6
- encode_weight: bfloat16 [512, 384], replicated, may hold values from -0.25 to 0.25
- conv_weight: bfloat16 [2, 1, 3456, 384], P('section', None, ('sy', 'sx')), may hold values from -0.109375 to 0.109375
- norm_gain: float32 [2, 1, 384], P('section'), may hold values from 0.1 to 1.9
- head_weight: bfloat16 [384, 256], replicated, may hold values from -0.3125 to 0.3125
- prior_logits: bfloat16 [4, 256, 256, 256], P('mb', 'sy', 'sx'), may hold values from -12 to 249
- target_bins: int32 [4, 256, 256], P('mb', 'sy', 'sx'), may hold values from 0 to 255
Outputs:
- section_features: bfloat16 [2, 4, 256, 256, 384], P('section', 'mb', 'sy', 'sx')
- head_step: float32 [384, 256], P('section')
- mean_loss: float32 [], replicated
All inputs are finite; a program needn't handle non-finite values.
Results may differ from a plain program's by a relative error of at most 0.008.
Values may be sent and summed in bfloat16 or wider, within the bound.
No kernel may reach another device: no remote copies, remote signals or barrier semaphores. Data moves between devices by JAX's collectives and lax.ppermute only.
A program may use at most 64 MiB of HBM per device.

v0:
```python
import jax
import jax.numpy as jnp
from jax import lax
from jax.sharding import PartitionSpec as P

FIRST_DILATION = 1
SECTION_FACTOR = 8


def norm_gelu(activations, gain):
    values = activations.astype(jnp.float32)
    center = jnp.mean(values, axis=-1, keepdims=True)
    offset = values - center
    spread = jnp.mean(offset * offset, axis=-1, keepdims=True)
    normed = offset * lax.rsqrt(spread + 1e-05) * gain
    return jax.nn.gelu(normed, approximate=False).astype(jnp.bfloat16)


def copies_to(block, axes, count):
    return lax.all_to_all(
        jnp.broadcast_to(block[None], (count,) + block.shape),
        axes,
        split_axis=0,
        concat_axis=0,
        tiled=True,
    )


def swap(block):
    return lax.ppermute(block, "section", [(0, 1), (1, 0)])


def patches_of(padded, rows, columns, step):
    channels = padded.shape[-1]
    windows = [
        padded[i * step : i * step + rows, j * step : j * step + columns]
        for i in range(3)
        for j in range(3)
    ]
    return jnp.concatenate(windows, axis=2).reshape(rows * columns, 9 * channels)


def split_two(value):
    high = value.astype(jnp.bfloat16)
    low = (value - high.astype(jnp.float32)).astype(jnp.bfloat16)
    return (high, low)


def per_device(
    frames, encode_weight, conv_weight, norm_gain, head_weight, prior_logits, target_bins
):
    section = lax.axis_index("section")
    first = section == 0
    parts_y = lax.axis_size("sy")
    parts_x = lax.axis_size("sx")
    parts_b = lax.axis_size("mb")
    side = frames.shape[1] // 2
    half = side // 2
    channels = encode_weight.shape[1]
    bins = head_weight.shape[1]
    near = FIRST_DILATION
    far = FIRST_DILATION * SECTION_FACTOR
    reach = near + far
    shard = conv_weight[0, 0]
    strip = copies_to(shard, "sx", parts_x).reshape(parts_x * shard.shape[0], channels)
    weight_own = lax.all_gather(strip, "sy", axis=0, tiled=True)
    gain_own = norm_gain[0, 0]
    gain_other = swap(gain_own)
    gain_0 = jnp.where(first, gain_own, gain_other)
    gain_1 = jnp.where(first, gain_other, gain_own)
    blocks = frames[0].reshape(side, 2, side, 2, frames.shape[3])
    kernel = encode_weight.reshape(2, 2, frames.shape[3], channels)
    encoded = jnp.einsum(
        "apbqc,pqco->abo", blocks, kernel, preferred_element_type=jnp.float32
    ).astype(jnp.bfloat16)
    outgoing = jnp.where(first, encoded[side - reach :], encoded[:reach])
    route = [(y, y + 1) for y in range(parts_y - 1)] + [
        (parts_y + y + 1, parts_y + y) for y in range(parts_y - 1)
    ]
    arrived = lax.ppermute(outgoing, ("section", "sy"), route)
    rows = jnp.where(
        first,
        jnp.concatenate([arrived, encoded[: half + reach]], axis=0),
        jnp.concatenate([encoded[half - reach :], arrived], axis=0),
    )
    forward = [(x, x + 1) for x in range(parts_x - 1)]
    backward = [(x + 1, x) for x in range(parts_x - 1)]
    left = lax.ppermute(rows[:, side - reach :], "sx", forward)
    right = lax.ppermute(rows[:, :reach], "sx", backward)
    haloed = jnp.concatenate([left, rows, right], axis=1)
    tall, wide = (half + 2 * far, side + 2 * far)
    hidden = norm_gelu(haloed, gain_0)
    patches = patches_of(hidden, tall, wide, near)
    weight_own, patches = lax.optimization_barrier((weight_own, patches))
    weight_other = swap(weight_own)
    weight_0 = jnp.where(first, weight_own, weight_other)
    weight_1 = jnp.where(first, weight_other, weight_own)
    summed = jnp.dot(patches, weight_0, preferred_element_type=jnp.float32)
    features_0 = (
        haloed[near : near + tall, near : near + wide].astype(jnp.float32)
        + summed.reshape(tall, wide, channels)
    ).astype(jnp.bfloat16)
    row_at = (
        lax.axis_index("sy") * side
        + section * half
        - far
        + lax.broadcasted_iota(jnp.int32, (tall, wide, 1), 0)
    )
    column_at = (
        lax.axis_index("sx") * side - far + lax.broadcasted_iota(jnp.int32, (tall, wide, 1), 1)
    )
    inside = (
        (row_at >= 0) & (row_at < side * parts_y) & (column_at >= 0) & (column_at < side * parts_x)
    )
    hidden = jnp.where(inside, norm_gelu(features_0, gain_1), jnp.bfloat16(0))
    patches = patches_of(hidden, half, side, far)
    summed = jnp.dot(patches, weight_1, preferred_element_type=jnp.float32)
    own_0 = features_0[far : far + half, far : far + side]
    own_1 = (own_0.astype(jnp.float32) + summed.reshape(half, side, channels)).astype(jnp.bfloat16)
    cells = half * side
    flat = own_1.reshape(cells, channels)
    prior = lax.dynamic_slice_in_dim(prior_logits[0], section * half, half, axis=0)
    target = lax.dynamic_slice_in_dim(target_bins[0], section * half, half, axis=0)
    logits = jnp.dot(flat, head_weight, preferred_element_type=jnp.float32)
    logits = logits + prior.reshape(cells, bins).astype(jnp.float32)
    row_top = jnp.max(logits, axis=1, keepdims=True)
    shifted = logits - row_top
    exp_terms = jnp.exp(shifted)
    exp_total = jnp.sum(exp_terms, axis=1, keepdims=True)
    softmax_rows = exp_terms / exp_total
    onehot = (target.reshape(cells, 1) == lax.broadcasted_iota(jnp.int32, (1, bins), 1)).astype(
        jnp.float32
    )
    loss_sum = jnp.sum(jnp.log(exp_total[:, 0]) - jnp.sum(shifted * onehot, axis=1))
    delta_rows = (softmax_rows - onehot).astype(jnp.bfloat16)
    gradient = lax.dot_general(
        flat, delta_rows, (((0,), (0,)), ((), ())), preferred_element_type=jnp.float32
    )
    slots = parts_x * parts_b
    slot_rows = channels // slots

    def with_loss(values, loss):
        high, low = split_two(loss)
        lane = lax.broadcasted_iota(jnp.int32, (1, bins), 1)
        row = jnp.where(lane == 0, high, jnp.where(lane == 1, low, jnp.bfloat16(0)))
        row = jnp.broadcast_to(row, values.shape[:-2] + (1, bins))
        return jnp.concatenate([values.astype(jnp.bfloat16), row], axis=-2)

    packed = with_loss(gradient.reshape(slots, slot_rows, bins), loss_sum)
    packed = lax.all_to_all(packed, ("sx", "mb"), split_axis=0, concat_axis=0, tiled=True)
    partial = jnp.sum(packed.astype(jnp.float32), axis=0)
    packed = with_loss(partial[:slot_rows], partial[slot_rows, 0] + partial[slot_rows, 1])
    packed = copies_to(packed, ("section", "sy"), 2 * parts_y)
    partial = jnp.sum(packed.astype(jnp.float32), axis=0)
    loss_all = partial[slot_rows, 0] + partial[slot_rows, 1]
    gathered = copies_to(partial[:slot_rows].astype(jnp.bfloat16), ("sx", "mb"), slots)
    gradient = gathered.reshape(channels, bins).astype(jnp.float32)
    scale = lax.rsqrt(jnp.mean(gradient * gradient) + 1e-06)
    own_rows = lax.dynamic_slice_in_dim(gradient, section * (channels // 2), channels // 2, axis=0)
    head_step = own_rows * scale
    mean_loss = loss_all / (parts_b * parts_y * parts_x * side * side)
    sent = swap(jnp.where(first, own_1, own_0))
    stacked = jnp.where(
        first, jnp.concatenate([own_0, sent], axis=0), jnp.concatenate([sent, own_1], axis=0)
    )[None, None]
    return (stacked, head_step, mean_loss)


def solution(mesh):
    placed = (
        P("mb", "sy", "sx", None),
        P(),
        P("section", None, ("sy", "sx"), None),
        P("section", None, None),
        P(),
        P("mb", "sy", "sx", None),
        P("mb", "sy", "sx"),
    )
    return jax.shard_map(
        per_device,
        mesh=mesh,
        in_specs=placed,
        out_specs=(P("section", "mb", "sy", "sx", None), P("section", None), P()),
        check_vma=False,
    )
```

profile of v0, /device:TPU:8, one launch (start us, length us, event | category | flops | bytes accessed | tf_op | source)
XLA Modules:
  0.0 193.8 jit_solution(5893310341925343398)
XLA Ops:
  7.2 2.1 %bitcast_convert_fusion = bf16[32,32,384]{2,1,0:T(8,128)(2,1)S(1)} fusion(bf16[2,2,128,384,1]{3,2,1,0,4:T(8,128)(2,1)} %bitcast.43, bf16[32,2,32,2,128]{4,3,2,1,0:T(2,128)(2,1)} %bitcast.42), kind=kOutput, calls=%fused_computation.66 | convolution fusion | flops 403046400 | bytes 2228224 | tf_op jit(solution)/shard_map/apbqc,pqco->abo/dot_general | solution.py:73
  9.3 3.6 %collective-permute-start = (bf16[9,32,384]{2,1,0:T(8,128)(2,1)S(1)}, bf16[9,32,384]{2,1,0:T(8,128)(2,1)S(1)}, u32[]{:S(2)}, u32[]{:S(2)}) collective-permute-start(bf16[9,32,384]{2,1,0:T(8,128)(2,1)S(1)} %slice_select_fusion), channel_id=1, source_target_pairs={{0,32},{32,64},{64,96},{96,128},{128,160},{160,192},{192,224},{288... | collective-permute-start | bytes 663560 | tf_op jit(solution)/shard_map/ppermute | solution.py:80
  13.1 7.4 %collective-permute-done = bf16[9,32,384]{2,1,0:T(8,128)(2,1)S(1)} collective-permute-done((bf16[9,32,384]{2,1,0:T(8,128)(2,1)S(1)}, bf16[9,32,384]{2,1,0:T(8,128)(2,1)S(1)}, u32[]{:S(2)}, u32[]{:S(2)}) %collective-permute-start) | collective-permute-done | bytes 221216 | tf_op jit(solution)/shard_map/ppermute | solution.py:80
  20.8 1.3 collective-permute-start.1
  22.1 1.3 collective-permute-start.2
  23.4 1.9 collective-permute-start.3
  26.1 11.6 %all-to-all-start = ((bf16[8,54,384]{2,1,0:T(8,128)(2,1)}), bf16[8,54,384]{2,1,0:T(8,128)(2,1)S(1)}, u32[]{:S(2)}, u32[]{:S(2)}) async-start(bf16[8,54,384]{2,1,0:T(8,128)(2,1)} %broadcast_in_dim.65), calls=%async_computation | async-start | bytes 688128 | tf_op jit(solution)/shard_map/all_to_all | solution.py:20
  38.5 1.7 convert_reduce_fusion
  41.1 10.9 %all-to-all-done = bf16[8,54,384]{2,1,0:T(8,128)(2,1)S(1)} async-done(((bf16[8,54,384]{2,1,0:T(8,128)(2,1)}), bf16[8,54,384]{2,1,0:T(8,128)(2,1)S(1)}, u32[]{:S(2)}, u32[]{:S(2)}) %all-to-all-start) | async-done | bytes 331808 | tf_op jit(solution)/shard_map/all_to_all | solution.py:20
  52.8 6.8 %fusion.7 = bf16[34,50,384]{2,1,0:T(8,128)(2,1)S(1)} fusion(bf16[34,50,384]{2,1,0:T(8,128)(2,1)S(1)} %get-tuple-element.14, f32[384]{0:T(512)S(1)} %get-tuple-element.25, f32[34,50]{1,0:T(8,128)S(1)} %add_rsqrt_fusion, f32[34,50]{1,0:T(8,128)S(1)} %broadcast_multiply_fusion), kind=kLoop, calls=%fused_computation.13 | loop fusion | flops 45043200 | bytes 2626336 | tf_op jit(solution)/shard_map/convert_element_type | solution.py:16
  59.6 1.2 slice_dynamic-update-slice_fusion.8
  60.8 1.6 slice_dynamic-update-slice_fusion.7
  62.4 1.6 slice_dynamic-update-slice_fusion.6
  64.1 1.2 slice_dynamic-update-slice_fusion.5
  65.2 1.6 slice_dynamic-update-slice_fusion.4
  66.9 1.6 slice_dynamic-update-slice_fusion.3
  68.5 1.2 slice_dynamic-update-slice_fusion.2
  69.7 1.6 slice_dynamic-update-slice_fusion.1
  71.3 1.6 slice_dynamic-update-slice_fusion
  72.9 22.1 %all-gather.2.cloned.1.call-done = bf16[3456,384]{1,0:T(8,128)(2,1)} async-done(((bf16[432,384]{1,0:T(8,128)(2,1)}), bf16[3456,384]{1,0:T(8,128)(2,1)}) %all-gather.2.cloned.1.call-update) | async-done | bytes 2654224 | tf_op jit(solution)/shard_map/all_gather | solution.py:66
  95.0 2.1 %collective-permute-start.4 = (bf16[3456,384]{1,0:T(8,128)(2,1)}, bf16[3456,384]{1,0:T(8,128)(2,1)}, u32[]{:S(2)}, u32[]{:S(2)}) collective-permute-start(bf16[3456,384]{1,0:T(8,128)(2,1)} %all-gather.2.cloned.1.call-done), channel_id=1, source_target_pairs={{0,256},{256,0},{1,257},{257,1},{2,258},{258,2},{3,259},{259,3},{4... | collective-permute-start | bytes 7962632 | tf_op jit(solution)/shard_map/ppermute | solution.py:30
  97.6 4.6 %collective-permute-done.4 = bf16[3456,384]{1,0:T(8,128)(2,1)} collective-permute-done((bf16[3456,384]{1,0:T(8,128)(2,1)}, bf16[3456,384]{1,0:T(8,128)(2,1)}, u32[]{:S(2)}, u32[]{:S(2)}) %collective-permute-start.4) | collective-permute-done | bytes 2654240 | tf_op jit(solution)/shard_map/ppermute | solution.py:30
  102.1 9.3 %fusion.25 = f32[1536,384]{1,0:T(8,128)S(1)} fusion(bf16[1536,3456]{1,0:T(8,128)(2,1)} %bitcast.6, bf16[3456,384]{1,0:T(8,128)(2,1)} %all-gather.2.cloned.1.call-done, bf16[3456,384]{1,0:T(8,128)(2,1)} %collective-permute-done.4, pred[]{:T(512)S(6)} %eq.50), kind=kOutput, calls=%fused_computation.37 | convolution fusion | flops 4078190592 | bytes 18284544 | tf_op jit(solution)/shard_map/dot_general | solution.py:98
  112.7 6.2 %fusion.47 = bf16[32,48,384]{2,1,0:T(8,128)(2,1)S(1)} fusion(bf16[32,48,384]{2,1,0:T(8,128)(2,1)S(1)} %get-tuple-element.12, f32[384]{0:T(512)S(1)} %get-tuple-element.24, f32[32,48]{1,0:T(8,128)S(1)} %add_rsqrt_fusion.1, f32[32,48]{1,0:T(8,128)S(1)} %broadcast_multiply_fusion.1, pred[32,48]{1,0:T(8,128)(4,1)S(1)} %and_and_fusion), kind=kLoop, calls=%fused_computation.69 | loop fusion | flops 41287680 | bytes 2374656 | tf_op jit(solution)/shard_map/jit(_where)/select_n | solution.py:115
  119.6 1.2 copy-done.6
  120.8 3.9 %broadcast_select_fusion = (bf16[16,32,384]{2,1,0:T(8,128)(2,1)S(1)}, bf16[16,32,384]{2,1,0:T(8,128)(2,1)S(1)}, bf16[1,1,16,32,384]{4,3,2,1,0:T(8,128)(2,1)S(1)}) fusion(pred[]{:T(512)S(6)} %eq.50, bf16[32,48,384]{2,1,0:T(8,128)(2,1)S(1)} %get-tuple-element.12, bf16[16,32,3456]{2,1,0:T(8,128)(2,1)S(1)} %slice_dynamic-update-slice_fusion.9, ...), kind=kOutput, calls=%fused_computation.100 | convolution fusion | flops 1361068032 | bytes 10421248 | tf_op jit(solution)/shard_map/dot_general | solution.py:117
  128.2 21.7 %all_to_all.20 = bf16[32,13,256]{2,1,0:T(8,128)(2,1)S(1)} all-to-all(bf16[32,13,256]{2,1,0:T(8,128)(2,1)S(1)} %copy.42), channel_id=1, replica_groups=mesh['section'=2,'sy'=8,'sx'=8,'mb'=4] {'sx','mb'}, dimensions={0} | all-to-all | bytes 425984 | tf_op jit(solution)/shard_map/all_to_all | solution.py:150
  152.5 5.3 %all-to-all-start.2 = ((bf16[16,13,256]{2,1,0:T(8,128)(2,1)}), bf16[16,13,256]{2,1,0:T(8,128)(2,1)S(1)}, u32[]{:S(2)}, u32[]{:S(2)}) async-start(bf16[16,13,256]{2,1,0:T(8,128)(2,1)} %broadcast_in_dim.75), calls=%async_computation.2 | async-start | bytes 262144 | tf_op jit(solution)/shard_map/all_to_all | solution.py:20
  157.8 2.0 %collective-permute-start.5 = (bf16[16,32,384]{2,1,0:T(8,128)(2,1)S(1)}, bf16[16,32,384]{2,1,0:T(8,128)(2,1)S(1)}, u32[]{:S(2)}, u32[]{:S(2)}) collective-permute-start(bf16[16,32,384]{2,1,0:T(8,128)(2,1)S(1)} %get-tuple-element.9), channel_id=1, source_target_pairs={{0,256},{256,0},{1,257},{257,1},{2,258},{258,2},{3,259},{259,3},{4... | collective-permute-start | bytes 1179656 | tf_op jit(solution)/shard_map/ppermute | solution.py:30
  159.9 6.2 %all-to-all-done.2 = bf16[16,13,256]{2,1,0:T(8,128)(2,1)S(1)} async-done(((bf16[16,13,256]{2,1,0:T(8,128)(2,1)}), bf16[16,13,256]{2,1,0:T(8,128)(2,1)S(1)}, u32[]{:S(2)}, u32[]{:S(2)}) %all-to-all-start.2) | async-done | bytes 106528 | tf_op jit(solution)/shard_map/all_to_all | solution.py:20
  166.8 3.9 %all-to-all-start.3 = ((bf16[32,12,256]{2,1,0:T(8,128)(2,1)}), bf16[32,12,256]{2,1,0:T(8,128)(2,1)S(1)}, u32[]{:S(2)}, u32[]{:S(2)}) async-start(bf16[32,12,256]{2,1,0:T(8,128)(2,1)} %broadcast_in_dim.76), calls=%async_computation.3 | async-start | bytes 524288 | tf_op jit(solution)/shard_map/all_to_all | solution.py:20
  173.6 10.0 %all-to-all-done.3 = bf16[32,12,256]{2,1,0:T(8,128)(2,1)S(1)} async-done(((bf16[32,12,256]{2,1,0:T(8,128)(2,1)}), bf16[32,12,256]{2,1,0:T(8,128)(2,1)S(1)}, u32[]{:S(2)}, u32[]{:S(2)}) %all-to-all-start.3) | async-done | bytes 196640 | tf_op jit(solution)/shard_map/all_to_all | solution.py:20
  (75 shorter events, 13.3 us)
Async XLA Ops:
  7.2 89.9 %copy-start = (bf16[1,32,32,256]{3,2,1,0:T(8,128)(2,1)S(1)}, bf16[1,32,32,256]{3,2,1,0:T(8,128)(2,1)}, u32[]{:S(2)}) copy-start(bf16[1,32,32,256]{3,2,1,0:T(8,128)(2,1)} %param.12) | copy-start | bytes 1572868
  9.3 14.1 %copy-start.5 = (f32[1,1,384]{2,1,0:T(1,128)S(1)}, f32[1,1,384]{2,1,0:T(1,128)}, u32[]{:S(2)}) copy-start(f32[1,1,384]{2,1,0:T(1,128)} %param.10) | copy-start | bytes 4612
  9.3 16.0 %copy-start.3 = (bf16[1,1,54,384]{3,2,1,0:T(8,128)(2,1)S(1)}, bf16[1,1,54,384]{3,2,1,0:T(8,128)(2,1)}, u32[]{:S(2)}) copy-start(bf16[1,1,54,384]{3,2,1,0:T(8,128)(2,1)} %param.9) | copy-start | bytes 124420
  9.3 11.1 %collective-permute-start = (bf16[9,32,384]{2,1,0:T(8,128)(2,1)S(1)}, bf16[9,32,384]{2,1,0:T(8,128)(2,1)S(1)}, u32[]{:S(2)}, u32[]{:S(2)}) collective-permute-start(bf16[9,32,384]{2,1,0:T(8,128)(2,1)S(1)} %slice_select_fusion), channel_id=1, source_target_pairs={{0,32},{32,64},{64,96},{96,128},{128,160},{160,192},{192,224},{288... | collective-permute-start | bytes 663560 | tf_op jit(solution)/shard_map/ppermute | solution.py:80
  20.8 17.0 %collective-permute-start.1 = (bf16[34,9,384]{2,1,0:T(8,128)(2,1)S(1)}, bf16[34,9,384]{2,1,0:T(8,128)(2,1)S(1)}, u32[]{:S(2)}, u32[]{:S(2)}) collective-permute-start(bf16[34,9,384]{2,1,0:T(8,128)(2,1)S(1)} %get-tuple-element.16), channel_id=1, source_target_pairs={{0,4},{4,8},{8,12},{12,16},{16,20},{20,24},{24,28},{1,5},{5,9},{9,... | collective-permute-start | bytes 705032 | tf_op jit(solution)/shard_map/ppermute | solution.py:88
  22.1 16.4 %collective-permute-start.2 = (bf16[34,9,384]{2,1,0:T(8,128)(2,1)S(1)}, bf16[34,9,384]{2,1,0:T(8,128)(2,1)}, u32[]{:S(2)}, u32[]{:S(2)}) collective-permute-start(bf16[34,9,384]{2,1,0:T(8,128)(2,1)S(1)} %get-tuple-element.17), channel_id=1, source_target_pairs={{4,0},{8,4},{12,8},{16,12},{20,16},{24,20},{28,24},{5,1},{9,5},{13... | collective-permute-start | bytes 705032 | tf_op jit(solution)/shard_map/ppermute | solution.py:89
  23.4 14.3 %collective-permute-start.3 = (f32[384]{0:T(512)S(1)}, f32[384]{0:T(512)S(1)}, u32[]{:S(2)}, u32[]{:S(2)}) collective-permute-start(f32[384]{0:T(512)S(1)} %reduce.1), channel_id=1, source_target_pairs={{0,256},{256,0},{1,257},{257,1},{2,258},{258,2},{3,259},{259,3},{4... | collective-permute-start | bytes 4616 | tf_op jit(solution)/shard_map/ppermute | solution.py:30
  26.1 25.8 %all-to-all-start = ((bf16[8,54,384]{2,1,0:T(8,128)(2,1)}), bf16[8,54,384]{2,1,0:T(8,128)(2,1)S(1)}, u32[]{:S(2)}, u32[]{:S(2)}) async-start(bf16[8,54,384]{2,1,0:T(8,128)(2,1)} %broadcast_in_dim.65), calls=%async_computation | async-start | bytes 688128 | tf_op jit(solution)/shard_map/all_to_all | solution.py:20
  37.7 57.3 %all-gather.2.cloned.1.call-start = ((), (), s32[]{:S(2)}) async-start(), calls=%async_computation.4 | async-start | bytes 2985984 | tf_op jit(solution)/shard_map/all_gather | solution.py:66
  37.8 0.8 copy-start.1
  71.3 26.1 %copy-start.4 = (s32[1,32,32]{2,1,0:T(8,128)S(1)}, s32[1,32,32]{2,1,0:T(8,128)}, u32[]{:S(2)}) copy-start(s32[1,32,32]{2,1,0:T(8,128)} %param.13) | copy-start | bytes 12292
  95.0 7.2 %collective-permute-start.4 = (bf16[3456,384]{1,0:T(8,128)(2,1)}, bf16[3456,384]{1,0:T(8,128)(2,1)}, u32[]{:S(2)}, u32[]{:S(2)}) collective-permute-start(bf16[3456,384]{1,0:T(8,128)(2,1)} %all-gather.2.cloned.1.call-done), channel_id=1, source_target_pairs={{0,256},{256,0},{1,257},{257,1},{2,258},{258,2},{3,259},{259,3},{4... | collective-permute-start | bytes 7962632 | tf_op jit(solution)/shard_map/ppermute | solution.py:30
  119.1 1.8 copy-start.6
  120.8 4.2 %copy-start.2 = (bf16[384,256]{1,0:T(8,128)(2,1)S(1)}, bf16[384,256]{1,0:T(8,128)(2,1)}, u32[]{:S(2)}) copy-start(bf16[384,256]{1,0:T(8,128)(2,1)} %param.11) | copy-start | bytes 589828
  152.5 13.5 %all-to-all-start.2 = ((bf16[16,13,256]{2,1,0:T(8,128)(2,1)}), bf16[16,13,256]{2,1,0:T(8,128)(2,1)S(1)}, u32[]{:S(2)}, u32[]{:S(2)}) async-start(bf16[16,13,256]{2,1,0:T(8,128)(2,1)} %broadcast_in_dim.75), calls=%async_computation.2 | async-start | bytes 262144 | tf_op jit(solution)/shard_map/all_to_all | solution.py:20
  157.8 12.9 %collective-permute-start.5 = (bf16[16,32,384]{2,1,0:T(8,128)(2,1)S(1)}, bf16[16,32,384]{2,1,0:T(8,128)(2,1)S(1)}, u32[]{:S(2)}, u32[]{:S(2)}) collective-permute-start(bf16[16,32,384]{2,1,0:T(8,128)(2,1)S(1)} %get-tuple-element.9), channel_id=1, source_target_pairs={{0,256},{256,0},{1,257},{257,1},{2,258},{258,2},{3,259},{259,3},{4... | collective-permute-start | bytes 1179656 | tf_op jit(solution)/shard_map/ppermute | solution.py:30
  166.8 16.8 %all-to-all-start.3 = ((bf16[32,12,256]{2,1,0:T(8,128)(2,1)}), bf16[32,12,256]{2,1,0:T(8,128)(2,1)S(1)}, u32[]{:S(2)}, u32[]{:S(2)}) async-start(bf16[32,12,256]{2,1,0:T(8,128)(2,1)} %broadcast_in_dim.76), calls=%async_computation.3 | async-start | bytes 524288 | tf_op jit(solution)/shard_map/all_to_all | solution.py:20
Sparse Core Ops, SparseCore 0:
  52.9 41.9 all-gather.1
where the time goes:
time: 195 us; the launch traced here: 194 us
  waiting for transfers between devices  61 us (31%)
  starting transfers between devices  33 us (17%)
  blocking collectives  21.7 us (11%)
  local copies, waits for them, and re-layouts  21 us (11%)
  other arithmetic  20.7 us (11%)
  between operations  20.3 us (10%)
  matrix products  16.1 us (8%)
    all_to_all x3, waiting for transfers between devices, copies_to(): lax.all_to_all(jnp.broadcast_to(block[None], (count,) + block.shape), axe...  27 us
    all_gather x1, waiting for transfers between devices, per_device(): weight_own = lax.all_gather(strip, 'sy', axis=0, tiled=True)  22.1 us
    all_to_all x1, blocking collectives, per_device(): lax.all_to_all(packed, ('sx', 'mb'), split_axis=0, concat_axis=0, tiled=T...  21.7 us
    all_to_all x3, starting transfers between devices, copies_to(): lax.all_to_all(jnp.broadcast_to(block[None], (count,) + block.shape), axe...  20.7 us
    unnamed x30, local copies, waits for them, and re-layouts  14.2 us
    dot_general x1, matrix products, per_device(): summed = jnp.dot(patches, weight_0, preferred_element_type=jnp.float32)  9.26 us
    ppermute x1, waiting for transfers between devices, per_device(): arrived = lax.ppermute(outgoing, ('section', 'sy'), route)  7.39 us
    convert_element_type x1, other arithmetic, norm_gelu(): return jax.nn.gelu(normed, approximate=False).astype(jnp.bfloat16)  6.79 us
  transfers between devices with their start and end apart: 10, of which 6 were waited for; matrix products, arithmetic and copies ran while one was open for 14% of the time, Pallas kernels for 0%

commit v1 on v0

--- a/solution.py
+++ b/solution.py
@@ -63,7 +63,9 @@
     reach = near + far
     shard = conv_weight[0, 0]
     strip = copies_to(shard, "sx", parts_x).reshape(parts_x * shard.shape[0], channels)
-    weight_own = lax.all_gather(strip, "sy", axis=0, tiled=True)
+    weight_own = jnp.concatenate(
+        lax.all_to_all(jnp.stack([strip] * lax.axis_size("sy")), "sy", 0, 0), axis=0
+    )
     gain_own = norm_gain[0, 0]
     gain_other = swap(gain_own)
     gain_0 = jnp.where(first, gain_own, gain_other)

time: 195 us -> 205 us (1.051)
  waiting for transfers between devices: 61 us -> 81 us
  between operations: 20.3 us -> 6.87 us
  starting transfers between devices: 33 us -> 41.3 us
  blocking collectives: 21.7 us -> 17.7 us
    all_to_all x0 -> x1, waiting for transfers between devices: none -> 41.9 us  [per_device(): lax.all_to_all(jnp.stack([strip] * lax.axis_size('sy')), 'sy', 0, 0)]
    all_gather x1 -> x0, waiting for transfers between devices: 22.1 us -> none  [per_device(): weight_own = lax.all_gather(strip, 'sy', axis=0, tiled=True)]
    all_to_all x0 -> x1, starting transfers between devices: none -> 8.75 us  [per_device(): lax.all_to_all(jnp.stack([strip] * lax.axis_size('sy')), 'sy', 0, 0)]
    all_to_all x1, blocking collectives: 21.7 us -> 17.7 us  [per_device(): lax.all_to_all(packed, ('sx', 'mb'), split_axis=0, concat_axis=0, tiled=T...]
    unnamed x30 -> x28, local copies, waits for them, and re-layouts: 14.2 us -> 13 us
  transfers between devices with their start and end apart: 10 -> 10, of which waited for: 6 -> 6; matrix products, arithmetic and copies ran while one was open for 14% -> 13% of each run, Pallas kernels for 0% -> 0%
where the time goes in v1:
time: 205 us; the launch traced here: 204 us
  waiting for transfers between devices  81 us (40%)
  starting transfers between devices  41.3 us (20%)
  local copies, waits for them, and re-layouts  20.7 us (10%)
  other arithmetic  20.7 us (10%)
  blocking collectives  17.7 us (9%)
  matrix products  16.1 us (8%)
  between operations  6.87 us (3%)
    all_to_all x1, waiting for transfers between devices, per_device(): lax.all_to_all(jnp.stack([strip] * lax.axis_size('sy')), 'sy', 0, 0)  41.9 us
    all_to_all x3, waiting for transfers between devices, copies_to(): lax.all_to_all(jnp.broadcast_to(block[None], (count,) + block.shape), axe...  27.1 us
    all_to_all x3, starting transfers between devices, copies_to(): lax.all_to_all(jnp.broadcast_to(block[None], (count,) + block.shape), axe...  20.3 us
    all_to_all x1, blocking collectives, per_device(): lax.all_to_all(packed, ('sx', 'mb'), split_axis=0, concat_axis=0, tiled=T...  17.7 us
    unnamed x28, local copies, waits for them, and re-layouts  13 us
    dot_general x1, matrix products, per_device(): summed = jnp.dot(patches, weight_0, preferred_element_type=jnp.float32)  9.26 us
    all_to_all x1, starting transfers between devices, per_device(): lax.all_to_all(jnp.stack([strip] * lax.axis_size('sy')), 'sy', 0, 0)  8.75 us
    ppermute x1, waiting for transfers between devices, per_device(): arrived = lax.ppermute(outgoing, ('section', 'sy'), route)  7.4 us
  transfers between devices with their start and end apart: 10, of which 6 were waited for; matrix products, arithmetic and copies ran while one was open for 13% of the time, Pallas kernels for 0%

profile of v1, /device:TPU:8, one launch (start us, length us, event | category | flops | bytes accessed | tf_op | source)
XLA Modules:
  0.0 204.3 jit_solution(6314150070524507794)
XLA Ops:
  0.7 2.1 %bitcast_convert_fusion = bf16[32,32,384]{2,1,0:T(8,128)(2,1)S(1)} fusion(bf16[2,2,128,384,1]{3,2,1,0,4:T(8,128)(2,1)} %bitcast.44, bf16[32,2,32,2,128]{4,3,2,1,0:T(2,128)(2,1)} %bitcast.43), kind=kOutput, calls=%fused_computation.66 | convolution fusion | flops 403046400 | bytes 2228224 | tf_op jit(solution)/shard_map/apbqc,pqco->abo/dot_general | solution.py:75
  2.8 3.6 %collective-permute-start = (bf16[9,32,384]{2,1,0:T(8,128)(2,1)S(1)}, bf16[9,32,384]{2,1,0:T(8,128)(2,1)S(1)}, u32[]{:S(2)}, u32[]{:S(2)}) collective-permute-start(bf16[9,32,384]{2,1,0:T(8,128)(2,1)S(1)} %slice_select_fusion), channel_id=1, source_target_pairs={{0,32},{32,64},{64,96},{96,128},{128,160},{160,192},{192,224},{288... | collective-permute-start | bytes 663560 | tf_op jit(solution)/shard_map/ppermute | solution.py:82
  6.5 7.4 %collective-permute-done = bf16[9,32,384]{2,1,0:T(8,128)(2,1)S(1)} collective-permute-done((bf16[9,32,384]{2,1,0:T(8,128)(2,1)S(1)}, bf16[9,32,384]{2,1,0:T(8,128)(2,1)S(1)}, u32[]{:S(2)}, u32[]{:S(2)}) %collective-permute-start) | collective-permute-done | bytes 221216 | tf_op jit(solution)/shard_map/ppermute | solution.py:82
  14.2 1.3 collective-permute-start.1
  15.6 1.3 collective-permute-start.2
  16.9 1.9 collective-permute-start.3
  19.6 11.5 %all-to-all-start = ((bf16[8,54,384]{2,1,0:T(8,128)(2,1)}), bf16[8,54,384]{2,1,0:T(8,128)(2,1)S(1)}, u32[]{:S(2)}, u32[]{:S(2)}) async-start(bf16[8,54,384]{2,1,0:T(8,128)(2,1)} %broadcast_in_dim.65), calls=%async_computation | async-start | bytes 688128 | tf_op jit(solution)/shard_map/all_to_all | solution.py:20
  31.9 1.7 convert_reduce_fusion
  34.5 10.9 %all-to-all-done = bf16[8,54,384]{2,1,0:T(8,128)(2,1)S(1)} async-done(((bf16[8,54,384]{2,1,0:T(8,128)(2,1)}), bf16[8,54,384]{2,1,0:T(8,128)(2,1)S(1)}, u32[]{:S(2)}, u32[]{:S(2)}) %all-to-all-start) | async-done | bytes 331808 | tf_op jit(solution)/shard_map/all_to_all | solution.py:20
  45.5 1.7 stack.3
  47.2 8.8 %all-to-all-start.1 = ((bf16[8,432,384]{2,1,0:T(8,128)(2,1)}), bf16[8,432,384]{2,1,0:T(8,128)(2,1)}, u32[]{:S(2)}, u32[]{:S(2)}) async-start(bf16[8,432,384]{2,1,0:T(8,128)(2,1)} %stack.3), calls=%async_computation.1 | async-start | bytes 5308416 | tf_op jit(solution)/shard_map/all_to_all | solution.py:67
  56.0 6.8 %fusion.7 = bf16[34,50,384]{2,1,0:T(8,128)(2,1)S(1)} fusion(bf16[34,50,384]{2,1,0:T(8,128)(2,1)S(1)} %get-tuple-element.14, f32[384]{0:T(512)S(1)} %get-tuple-element.25, f32[34,50]{1,0:T(8,128)S(1)} %add_rsqrt_fusion, f32[34,50]{1,0:T(8,128)S(1)} %broadcast_multiply_fusion), kind=kLoop, calls=%fused_computation.13 | loop fusion | flops 45043200 | bytes 2626336 | tf_op jit(solution)/shard_map/convert_element_type | solution.py:16
  62.8 1.2 slice_dynamic-update-slice_fusion.8
  64.0 1.6 slice_dynamic-update-slice_fusion.7
  65.6 1.6 slice_dynamic-update-slice_fusion.6
  68.4 1.6 slice_dynamic-update-slice_fusion.4
  70.0 1.6 slice_dynamic-update-slice_fusion.3
  71.7 1.2 slice_dynamic-update-slice_fusion.2
  72.9 1.6 slice_dynamic-update-slice_fusion.1
  74.5 1.6 slice_dynamic-update-slice_fusion
  76.1 41.9 %all-to-all-done.1 = bf16[8,432,384]{2,1,0:T(8,128)(2,1)} async-done(((bf16[8,432,384]{2,1,0:T(8,128)(2,1)}), bf16[8,432,384]{2,1,0:T(8,128)(2,1)}, u32[]{:S(2)}, u32[]{:S(2)}) %all-to-all-start.1) | async-done | bytes 2654240 | tf_op jit(solution)/shard_map/all_to_all | solution.py:67
  118.0 2.1 %collective-permute-start.4 = (bf16[3456,384]{1,0:T(8,128)(2,1)}, bf16[3456,384]{1,0:T(8,128)(2,1)}, u32[]{:S(2)}, u32[]{:S(2)}) collective-permute-start(bf16[3456,384]{1,0:T(8,128)(2,1)} %bitcast.6), channel_id=1, source_target_pairs={{0,256},{256,0},{1,257},{257,1},{2,258},{258,2},{3,259},{259,3},{4... | collective-permute-start | bytes 7962632 | tf_op jit(solution)/shard_map/ppermute | solution.py:30
  120.6 4.6 %collective-permute-done.4 = bf16[3456,384]{1,0:T(8,128)(2,1)} collective-permute-done((bf16[3456,384]{1,0:T(8,128)(2,1)}, bf16[3456,384]{1,0:T(8,128)(2,1)}, u32[]{:S(2)}, u32[]{:S(2)}) %collective-permute-start.4) | collective-permute-done | bytes 2654240 | tf_op jit(solution)/shard_map/ppermute | solution.py:30
  125.2 9.3 %fusion.25 = f32[1536,384]{1,0:T(8,128)S(1)} fusion(bf16[1536,3456]{1,0:T(8,128)(2,1)} %bitcast.7, bf16[3456,384]{1,0:T(8,128)(2,1)} %bitcast.6, bf16[3456,384]{1,0:T(8,128)(2,1)} %collective-permute-done.4, pred[]{:T(512)S(6)} %eq.50), kind=kOutput, calls=%fused_computation.37 | convolution fusion | flops 4078190592 | bytes 18284544 | tf_op jit(solution)/shard_map/dot_general | solution.py:100
  135.7 6.3 %fusion.47 = bf16[32,48,384]{2,1,0:T(8,128)(2,1)S(1)} fusion(bf16[32,48,384]{2,1,0:T(8,128)(2,1)S(1)} %get-tuple-element.12, f32[384]{0:T(512)S(1)} %get-tuple-element.24, f32[32,48]{1,0:T(8,128)S(1)} %add_rsqrt_fusion.1, f32[32,48]{1,0:T(8,128)S(1)} %broadcast_multiply_fusion.1, pred[32,48]{1,0:T(8,128)(4,1)S(1)} %and_and_fusion), kind=kLoop, calls=%fused_computation.69 | loop fusion | flops 41287680 | bytes 2374656 | tf_op jit(solution)/shard_map/jit(_where)/select_n | solution.py:117
  142.6 3.9 %broadcast_select_fusion = (bf16[16,32,384]{2,1,0:T(8,128)(2,1)S(1)}, bf16[16,32,384]{2,1,0:T(8,128)(2,1)S(1)}, bf16[1,1,16,32,384]{4,3,2,1,0:T(8,128)(2,1)S(1)}) fusion(pred[]{:T(512)S(6)} %eq.50, bf16[32,48,384]{2,1,0:T(8,128)(2,1)S(1)} %get-tuple-element.12, bf16[16,32,3456]{2,1,0:T(8,128)(2,1)S(1)} %slice_dynamic-update-slice_fusion.9, ...), kind=kOutput, calls=%fused_computation.100 | convolution fusion | flops 1361068032 | bytes 10421248 | tf_op jit(solution)/shard_map/dot_general | solution.py:119
  150.0 17.7 %all_to_all.25 = bf16[32,13,256]{2,1,0:T(8,128)(2,1)S(1)} all-to-all(bf16[32,13,256]{2,1,0:T(8,128)(2,1)S(1)} %copy.42), channel_id=1, replica_groups=mesh['section'=2,'sy'=8,'sx'=8,'mb'=4] {'sx','mb'}, dimensions={0} | all-to-all | bytes 425984 | tf_op jit(solution)/shard_map/all_to_all | solution.py:152
  170.3 4.8 %all-to-all-start.3 = ((bf16[16,13,256]{2,1,0:T(8,128)(2,1)}), bf16[16,13,256]{2,1,0:T(8,128)(2,1)S(1)}, u32[]{:S(2)}, u32[]{:S(2)}) async-start(bf16[16,13,256]{2,1,0:T(8,128)(2,1)} %broadcast_in_dim.75), calls=%async_computation.3 | async-start | bytes 262144 | tf_op jit(solution)/shard_map/all_to_all | solution.py:20
  175.2 2.1 %collective-permute-start.5 = (bf16[16,32,384]{2,1,0:T(8,128)(2,1)S(1)}, bf16[16,32,384]{2,1,0:T(8,128)(2,1)S(1)}, u32[]{:S(2)}, u32[]{:S(2)}) collective-permute-start(bf16[16,32,384]{2,1,0:T(8,128)(2,1)S(1)} %get-tuple-element.9), channel_id=1, source_target_pairs={{0,256},{256,0},{1,257},{257,1},{2,258},{258,2},{3,259},{259,3},{4... | collective-permute-start | bytes 1179656 | tf_op jit(solution)/shard_map/ppermute | solution.py:30
  177.3 6.2 %all-to-all-done.3 = bf16[16,13,256]{2,1,0:T(8,128)(2,1)S(1)} async-done(((bf16[16,13,256]{2,1,0:T(8,128)(2,1)}), bf16[16,13,256]{2,1,0:T(8,128)(2,1)S(1)}, u32[]{:S(2)}, u32[]{:S(2)}) %all-to-all-start.3) | async-done | bytes 106528 | tf_op jit(solution)/shard_map/all_to_all | solution.py:20
  184.2 3.9 %all-to-all-start.4 = ((bf16[32,12,256]{2,1,0:T(8,128)(2,1)}), bf16[32,12,256]{2,1,0:T(8,128)(2,1)S(1)}, u32[]{:S(2)}, u32[]{:S(2)}) async-start(bf16[32,12,256]{2,1,0:T(8,128)(2,1)} %broadcast_in_dim.76), calls=%async_computation.4 | async-start | bytes 524288 | tf_op jit(solution)/shard_map/all_to_all | solution.py:20
  191.0 10.0 %all-to-all-done.4 = bf16[32,12,256]{2,1,0:T(8,128)(2,1)S(1)} async-done(((bf16[32,12,256]{2,1,0:T(8,128)(2,1)}), bf16[32,12,256]{2,1,0:T(8,128)(2,1)S(1)}, u32[]{:S(2)}, u32[]{:S(2)}) %all-to-all-start.4) | async-done | bytes 196640 | tf_op jit(solution)/shard_map/all_to_all | solution.py:20
  (73 shorter events, 13.7 us)
Async XLA Ops:
  0.6 119.5 %copy-start = (bf16[1,32,32,256]{3,2,1,0:T(8,128)(2,1)S(1)}, bf16[1,32,32,256]{3,2,1,0:T(8,128)(2,1)}, u32[]{:S(2)}) copy-start(bf16[1,32,32,256]{3,2,1,0:T(8,128)(2,1)} %param.12) | copy-start | bytes 1572868
  2.8 14.1 %copy-start.5 = (f32[1,1,384]{2,1,0:T(1,128)S(1)}, f32[1,1,384]{2,1,0:T(1,128)}, u32[]{:S(2)}) copy-start(f32[1,1,384]{2,1,0:T(1,128)} %param.10) | copy-start | bytes 4612
  2.8 16.1 %copy-start.3 = (bf16[1,1,54,384]{3,2,1,0:T(8,128)(2,1)S(1)}, bf16[1,1,54,384]{3,2,1,0:T(8,128)(2,1)}, u32[]{:S(2)}) copy-start(bf16[1,1,54,384]{3,2,1,0:T(8,128)(2,1)} %param.9) | copy-start | bytes 124420
  2.8 11.1 %collective-permute-start = (bf16[9,32,384]{2,1,0:T(8,128)(2,1)S(1)}, bf16[9,32,384]{2,1,0:T(8,128)(2,1)S(1)}, u32[]{:S(2)}, u32[]{:S(2)}) collective-permute-start(bf16[9,32,384]{2,1,0:T(8,128)(2,1)S(1)} %slice_select_fusion), channel_id=1, source_target_pairs={{0,32},{32,64},{64,96},{96,128},{128,160},{160,192},{192,224},{288... | collective-permute-start | bytes 663560 | tf_op jit(solution)/shard_map/ppermute | solution.py:82
  14.2 16.9 %collective-permute-start.1 = (bf16[34,9,384]{2,1,0:T(8,128)(2,1)S(1)}, bf16[34,9,384]{2,1,0:T(8,128)(2,1)S(1)}, u32[]{:S(2)}, u32[]{:S(2)}) collective-permute-start(bf16[34,9,384]{2,1,0:T(8,128)(2,1)S(1)} %get-tuple-element.16), channel_id=1, source_target_pairs={{0,4},{4,8},{8,12},{12,16},{16,20},{20,24},{24,28},{1,5},{5,9},{9,... | collective-permute-start | bytes 705032 | tf_op jit(solution)/shard_map/ppermute | solution.py:90
  15.6 16.4 %collective-permute-start.2 = (bf16[34,9,384]{2,1,0:T(8,128)(2,1)S(1)}, bf16[34,9,384]{2,1,0:T(8,128)(2,1)}, u32[]{:S(2)}, u32[]{:S(2)}) collective-permute-start(bf16[34,9,384]{2,1,0:T(8,128)(2,1)S(1)} %get-tuple-element.17), channel_id=1, source_target_pairs={{4,0},{8,4},{12,8},{16,12},{20,16},{24,20},{28,24},{5,1},{9,5},{13... | collective-permute-start | bytes 705032 | tf_op jit(solution)/shard_map/ppermute | solution.py:91
  16.9 14.3 %collective-permute-start.3 = (f32[384]{0:T(512)S(1)}, f32[384]{0:T(512)S(1)}, u32[]{:S(2)}, u32[]{:S(2)}) collective-permute-start(f32[384]{0:T(512)S(1)} %reduce.1), channel_id=1, source_target_pairs={{0,256},{256,0},{1,257},{257,1},{2,258},{258,2},{3,259},{259,3},{4... | collective-permute-start | bytes 4616 | tf_op jit(solution)/shard_map/ppermute | solution.py:30
  19.6 25.8 %all-to-all-start = ((bf16[8,54,384]{2,1,0:T(8,128)(2,1)}), bf16[8,54,384]{2,1,0:T(8,128)(2,1)S(1)}, u32[]{:S(2)}, u32[]{:S(2)}) async-start(bf16[8,54,384]{2,1,0:T(8,128)(2,1)} %broadcast_in_dim.65), calls=%async_computation | async-start | bytes 688128 | tf_op jit(solution)/shard_map/all_to_all | solution.py:20
  31.2 0.8 copy-start.1
  47.2 70.7 %all-to-all-start.1 = ((bf16[8,432,384]{2,1,0:T(8,128)(2,1)}), bf16[8,432,384]{2,1,0:T(8,128)(2,1)}, u32[]{:S(2)}, u32[]{:S(2)}) async-start(bf16[8,432,384]{2,1,0:T(8,128)(2,1)} %stack.3), calls=%async_computation.1 | async-start | bytes 5308416 | tf_op jit(solution)/shard_map/all_to_all | solution.py:67
  74.5 45.9 %copy-start.4 = (s32[1,32,32]{2,1,0:T(8,128)S(1)}, s32[1,32,32]{2,1,0:T(8,128)}, u32[]{:S(2)}) copy-start(s32[1,32,32]{2,1,0:T(8,128)} %param.13) | copy-start | bytes 12292
  118.0 7.2 %collective-permute-start.4 = (bf16[3456,384]{1,0:T(8,128)(2,1)}, bf16[3456,384]{1,0:T(8,128)(2,1)}, u32[]{:S(2)}, u32[]{:S(2)}) collective-permute-start(bf16[3456,384]{1,0:T(8,128)(2,1)} %bitcast.6), channel_id=1, source_target_pairs={{0,256},{256,0},{1,257},{257,1},{2,258},{258,2},{3,259},{259,3},{4... | collective-permute-start | bytes 7962632 | tf_op jit(solution)/shard_map/ppermute | solution.py:30
  142.6 4.2 %copy-start.2 = (bf16[384,256]{1,0:T(8,128)(2,1)S(1)}, bf16[384,256]{1,0:T(8,128)(2,1)}, u32[]{:S(2)}) copy-start(bf16[384,256]{1,0:T(8,128)(2,1)} %param.11) | copy-start | bytes 589828
  170.3 13.1 %all-to-all-start.3 = ((bf16[16,13,256]{2,1,0:T(8,128)(2,1)}), bf16[16,13,256]{2,1,0:T(8,128)(2,1)S(1)}, u32[]{:S(2)}, u32[]{:S(2)}) async-start(bf16[16,13,256]{2,1,0:T(8,128)(2,1)} %broadcast_in_dim.75), calls=%async_computation.3 | async-start | bytes 262144 | tf_op jit(solution)/shard_map/all_to_all | solution.py:20
  175.2 12.9 %collective-permute-start.5 = (bf16[16,32,384]{2,1,0:T(8,128)(2,1)S(1)}, bf16[16,32,384]{2,1,0:T(8,128)(2,1)S(1)}, u32[]{:S(2)}, u32[]{:S(2)}) collective-permute-start(bf16[16,32,384]{2,1,0:T(8,128)(2,1)S(1)} %get-tuple-element.9), channel_id=1, source_target_pairs={{0,256},{256,0},{1,257},{257,1},{2,258},{258,2},{3,259},{259,3},{4... | collective-permute-start | bytes 1179656 | tf_op jit(solution)/shard_map/ppermute | solution.py:30
  184.2 16.8 %all-to-all-start.4 = ((bf16[32,12,256]{2,1,0:T(8,128)(2,1)}), bf16[32,12,256]{2,1,0:T(8,128)(2,1)S(1)}, u32[]{:S(2)}, u32[]{:S(2)}) async-start(bf16[32,12,256]{2,1,0:T(8,128)(2,1)} %broadcast_in_dim.76), calls=%async_computation.4 | async-start | bytes 524288 | tf_op jit(solution)/shard_map/all_to_all | solution.py:20
